TPU v7x, 32 devices: a whole 2x2x4 slice. The times are simulated.
32 devices in a mesh: vec: 4 (over y, x), orb: 8 (over z, core).
Axes of the slice: x: 2, y: 2, z: 4, core: 2. Of those that a mesh axis runs over, the one named last changes fastest.
Arguments:
- chol_occ: float32 [44, 96, 1056], P('vec', 'orb'), may hold values from -6 to 6
- chol_vir: float32 [44, 960, 1056], P('vec', 'orb'), may hold values from -6 to 6
- singles: float32 [96, 960], P('orb'), may hold values from -0.6 to 0.6
Outputs:
- dressed_vir: float32 [44, 960, 1056], P('vec', 'orb')
- dressed_ov: float32 [44, 96, 960], P(None, 'orb', 'vec')
- fock_ov: float32 [96, 960], P('orb')
All inputs are finite; a program needn't handle non-finite values.
Results may differ from a plain program's by a relative error of at most 0.000086.
Values sent between devices are 32-bit elements; how exact they have to be, the bound alone decides.
A program may use at most 64 MiB of HBM per device.

v0:
```python
import jax
import jax.numpy as jnp
from jax import lax
from jax.sharding import PartitionSpec as P


def dress_right(matrix_rows, amplitudes):
    occ_width = amplitudes.shape[0]
    occ_cols = matrix_rows[:, :, :occ_width]
    extra_term = jnp.einsum("qrj,ja->qra", occ_cols, amplitudes, precision=lax.Precision.HIGHEST)
    return jnp.concatenate([occ_cols, matrix_rows[:, :, occ_width:] + extra_term], axis=2)


def dress_left(vir_rows, occ_all, amp_cols):
    return vir_rows - jnp.einsum("qin,ia->qan", occ_all, amp_cols, precision=lax.Precision.HIGHEST)


def shards(chol_occ, chol_vir, singles):
    amplitudes = lax.all_gather(singles, "orb", axis=0, tiled=True)
    occ_width = amplitudes.shape[0]
    vir_local = chol_vir.shape[1]
    vir_start = lax.axis_index("orb") * vir_local
    amp_cols = lax.dynamic_slice_in_dim(amplitudes, vir_start, vir_local, 1)
    occ_all = lax.all_gather(chol_occ, "orb", axis=1, tiled=True)
    dressed_vir = dress_right(dress_left(chol_vir, occ_all, amp_cols), amplitudes)
    dressed_occ = dress_right(chol_occ, amplitudes)
    local_rows = chol_occ.shape[1]
    first_row = lax.axis_index("orb") * local_rows
    row_ids = lax.broadcasted_iota(jnp.int32, (local_rows, chol_occ.shape[2]), 0) + first_row
    col_ids = lax.broadcasted_iota(jnp.int32, (local_rows, chol_occ.shape[2]), 1)
    diag_mask = jnp.where(row_ids == col_ids, 1.0, 0.0).astype(jnp.float32)
    traces_local = jnp.sum(chol_occ * diag_mask[None], axis=(1, 2))
    traces = lax.psum(traces_local, "orb")
    ov_block = dressed_occ[:, :, occ_width:]
    total_vectors = chol_occ.shape[0] * lax.axis_size("vec")
    fock_part = (
        jnp.einsum("q,qia->ia", traces, ov_block, precision=lax.Precision.HIGHEST) / total_vectors
    )
    fock_ov = lax.psum(fock_part, "vec")
    pair_blocks = lax.all_to_all(ov_block, "vec", split_axis=2, concat_axis=0, tiled=True)
    return (dressed_vir, pair_blocks, fock_ov)


def solution(mesh):
    return jax.shard_map(
        shards,
        mesh=mesh,
        in_specs=(P("vec", "orb", None), P("vec", "orb", None), P("orb", None)),
        out_specs=(P("vec", "orb", None), P(None, "orb", "vec"), P("orb", None)),
        check_vma=False,
    )
```

profile of v0, /device:TPU:0, one launch (start us, length us, event | category | flops | bytes accessed | tf_op | source)
XLA Modules:
  0.0 127.6 jit_solution(5254257879419233849)
XLA Ops:
  7.2 0.0 all-gather.3.cloned.1.call-start
  7.2 2.3 %copy.10 = f32[11,12,1056]{2,0,1:T(8,128)} copy(f32[11,12,1056]{2,1,0:T(8,128)} %param.3) | data formatting | bytes 1115136 | tf_op args[0]
  9.5 0.0 all-gather.3.cloned.1.call-update
  9.5 16.7 %all-gather = f32[8,12,960]{2,1,0:T(8,128)S(1)} all-gather(f32[1,12,960]{2,1,0:T(8,128)} %bitcast.22), channel_id=1, replica_groups=mesh['vec'=4,'orb'=8] {'orb'}, dimensions={0}, use_global_device_ids=true | all-gather | bytes 414720 | tf_op jit(solution)/shard_map/all_gather | solution.py:19
  26.3 1.9 %convolution_add_fusion = f32[11,12,960]{2,1,0:T(8,128)S(1)} fusion(f32[96,960,1]{1,0,2:T(8,128)S(1)} %reshape.23, f32[11,12,1056]{2,1,0:T(8,128)} %param.3), kind=kOutput, calls=%fused_computation.4 | convolution fusion | flops 146108160 | bytes 1433088 | tf_op jit(solution)/shard_map/qrj,ja->qra/dot_general | solution.py:10
  28.2 6.0 %copy.13 = f32[11,12,960]{1,0,2:T(8,128)} copy(f32[11,12,960]{2,1,0:T(8,128)S(1)} %convolution_add_fusion) | data formatting | bytes 1013760 | tf_op jit(solution)/shard_map/add | solution.py:11
  34.2 0.0 copy-start
  34.2 6.5 %reshape.27 = f32[4,1,31680]{2,1,0:T(1,128)} reshape(f32[960,11,12]{2,1,0:T(8,128)} %bitcast.20) | data formatting | bytes 1013760
  40.7 0.1 fusion.4
  40.8 0.0 copy-done
  40.8 0.2 multiply_reduce_fusion
  41.0 3.7 %all-to-all-start = ((f32[4,1,31680]{2,1,0:T(1,128)}), f32[4,1,31680]{2,1,0:T(1,128)S(1)}, u32[]{:S(2)}, u32[]{:S(2)}) async-start(f32[4,1,31680]{2,1,0:T(1,128)} %reshape.27), calls=%async_computation | async-start | bytes 1015808 | tf_op jit(solution)/shard_map/all_to_all | solution.py:40
  44.7 19.3 %psum.14 = f32[11]{0:T(128)S(1)} all-reduce(f32[11]{0:T(128)S(1)} %multiply_reduce_fusion), channel_id=1, replica_groups=mesh['vec'=4,'orb'=8] {'orb'}, use_global_device_ids=true, to_apply=%region_1.2 | all-reduce | flops 11 | bytes 88 | tf_op jit(solution)/shard_map/psum | solution.py:33
  64.0 0.8 fusion.1
  64.9 17.7 %psum.15 = f32[12,960]{1,0:T(8,128)} all-reduce(f32[12,960]{1,0:T(8,128)S(1)} %bitcast_multiply_fusion), channel_id=1, replica_groups=mesh['vec'=4,'orb'=8] {'vec'}, use_global_device_ids=true, to_apply=%region_2.3 | all-reduce | flops 11520 | bytes 92160 | tf_op jit(solution)/shard_map/psum | solution.py:39
  82.5 0.0 all-to-all-done
  82.5 0.5 broadcast.18
  83.0 2.1 %reduce = f32[4,31680]{1,0:T(4,128)S(1)} reduce(f32[4,1,31680]{2,1,0:T(1,128)S(1)} %all-to-all-done, f32[]{:T(128)} %broadcast.18), dimensions={1}, to_apply=%all_to_all.13.reduce_sub_computation | reduce | bytes 1013764 | tf_op jit(solution)/shard_map/all_to_all | solution.py:40
  85.2 6.0 %reshape.28 = f32[960,11,12]{2,1,0:T(8,128)} reshape(f32[4,31680]{1,0:T(4,128)S(1)} %reduce) | data formatting | bytes 1013760
  91.2 6.2 %copy.14 = f32[11,12,4,240]{3,0,2,1:T(8,128)S(1)} copy(f32[11,12,4,240]{1,0,3,2:T(8,128)} %bitcast.19) | data formatting | bytes 1013760 | tf_op jit(solution)/shard_map/all_to_all | solution.py:40
  97.4 0.9 all_to_all.16
  98.3 0.0 all-gather.3.cloned.1.call-done
  98.3 14.5 %bitcast_subtract_fusion = f32[11,120,1056]{1,2,0:T(8,128)S(1)} fusion(f32[11,120,1056]{1,2,0:T(8,128)} %param.4, f32[11,96,1056]{2,0,1:T(8,128)} %all-gather.3.cloned.1.call-done, f32[96,960]{1,0:T(8,128)S(1)} %reshape.21, s32[]{:T(128)S(6)} %select_n.11), kind=kOutput, calls=%fused_computation.1 | convolution fusion | flops 1607189760 | bytes 15661060 | tf_op jit(solution)/shard_map/qin,ia->qan/dot_general | solution.py:15
  112.9 4.7 %slice_add_fusion = f32[11,120,960]{1,2,0:T(8,128)S(1)} fusion(f32[11,120,1056]{1,2,0:T(8,128)S(1)} %bitcast_subtract_fusion, f32[96,960,1]{1,0,2:T(8,128)S(1)} %reshape.23), kind=kOutput, calls=%fused_computation.2 | convolution fusion | flops 1461081600 | bytes 11013120 | tf_op jit(solution)/shard_map/qrj,ja->qra/dot_general | solution.py:10
  117.6 3.2 %pad_maximum_fusion = f32[11,120,1056]{1,2,0:T(8,128)} fusion(f32[11,120,960]{1,2,0:T(8,128)S(1)} %slice_add_fusion, f32[11,120,96]{1,2,0:T(8,128)S(1)} %slice.16), kind=kLoop, calls=%fused_computation | loop fusion | flops 1393920 | bytes 11151360 | tf_op jit(solution)/shard_map/concatenate | solution.py:11
  (5 shorter events, 0.1 us)
Async XLA Ops:
  7.2 91.1 %all-gather.3.cloned.1.call-start = ((), (), s32[]{:S(2)}) async-start(), calls=%async_computation.1 | async-start | bytes 7962624 | tf_op jit(solution)/shard_map/all_gather | solution.py:24
  34.2 6.6 %copy-start = (f32[11,12,1056]{2,1,0:T(8,128)S(1)}, f32[11,12,1056]{2,1,0:T(8,128)}, u32[]{:S(2)}) copy-start(f32[11,12,1056]{2,1,0:T(8,128)} %param.3) | copy-start | bytes 1672708
  41.0 41.6 %all-to-all-start = ((f32[4,1,31680]{2,1,0:T(1,128)}), f32[4,1,31680]{2,1,0:T(1,128)S(1)}, u32[]{:S(2)}, u32[]{:S(2)}) async-start(f32[4,1,31680]{2,1,0:T(1,128)} %reshape.27), calls=%async_computation | async-start | bytes 1015808 | tf_op jit(solution)/shard_map/all_to_all | solution.py:40
Sparse Core Ops, SparseCore 0:
  10.2 74.4 all-gather.2
where the time goes:
time: 128 us
  blocking collectives  53.7 us (42%)
  local copies, waits for them, and re-layouts  28.5 us (22%)
  matrix products  22 us (17%)
  between operations  14.1 us (11%)
  other arithmetic  5.58 us (4%)
  starting transfers between devices  3.76 us (3%)
    psum x1, blocking collectives, shards(): traces = lax.psum(traces_local, 'orb')  19.3 us
    psum x1, blocking collectives, shards(): fock_ov = lax.psum(fock_part, 'vec')  17.7 us
    all_gather x1, blocking collectives, shards(): amplitudes = lax.all_gather(singles, 'orb', axis=0, tiled=True)  16.7 us
    unnamed x7, local copies, waits for them, and re-layouts  14.9 us
    dot_general x1, matrix products, dress_left(): jnp.einsum('qin,ia->qan', occ_all, amp_cols, precision=lax.Precision.HIGH...  14.5 us
    all_to_all x3, local copies, waits for them, and re-layouts, shards(): lax.all_to_all(ov_block, 'vec', split_axis=2, concat_axis=0, tiled=True)  7.57 us
    dot_general x2, matrix products, dress_right(): jnp.einsum('qrj,ja->qra', occ_cols, amplitudes, precision=lax.Precision.H...  6.66 us
    add x1, local copies, waits for them, and re-layouts, dress_right(): matrix_rows[:, :, occ_width:] + extra_term  5.96 us
  transfers between devices with their start and end apart: 2, of which 0 were waited for; matrix products, arithmetic and copies ran while one was open for 24% of the time, Pallas kernels for 0%

commit v1 on v0

--- a/solution.py
+++ b/solution.py
@@ -2,6 +2,28 @@
 import jax.numpy as jnp
 from jax import lax
 from jax.sharding import PartitionSpec as P
+
+
+def joined_along(tiles, dim):
+    tiles = jnp.moveaxis(tiles, 0, dim)
+    lengths = tiles.shape
+    return tiles.reshape(*lengths[:dim], lengths[dim] * lengths[dim + 1], *lengths[dim + 2 :])
+
+
+def collected_by_bits(value, axis):
+    peers = lax.axis_size(axis)
+    parts = value[None]
+    for level in range(peers.bit_length() - 1):
+        apart = 1 << level
+        theirs = lax.ppermute(parts, axis, [(i, i ^ apart) for i in range(peers)])
+        both = jnp.stack([parts, theirs])
+        upper = lax.axis_index(axis) >> level & 1
+        parts = jnp.where(upper == 0, both, both[::-1]).reshape(-1, *value.shape)
+    return parts
+
+
+def collect(x, axis, dim):
+    return joined_along(collected_by_bits(x, axis), dim)
 
 
 def dress_right(matrix_rows, amplitudes):
@@ -16,7 +38,7 @@
 
 
 def shards(chol_occ, chol_vir, singles):
-    amplitudes = lax.all_gather(singles, "orb", axis=0, tiled=True)
+    amplitudes = collect(singles, "orb", 0)
     occ_width = amplitudes.shape[0]
     vir_local = chol_vir.shape[1]
     vir_start = lax.axis_index("orb") * vir_local

time: 128 us -> 142 us (1.11)
  the two profiles are of different devices: /device:TPU:0 before, /device:TPU:16 now
where the time goes in v1:
time: 142 us
  blocking collectives  58.3 us (41%)
  local copies, waits for them, and re-layouts  28.4 us (20%)
  matrix products  22 us (15%)
  between operations  14.2 us (10%)
  other arithmetic  7.79 us (5%)
  starting transfers between devices  5.58 us (4%)
  waiting for transfers between devices  5.44 us (4%)
    psum x1, blocking collectives, shards(): traces = lax.psum(traces_local, 'orb')  40.3 us
    psum x1, blocking collectives, shards(): fock_ov = lax.psum(fock_part, 'vec')  18 us
    unnamed x3, local copies, waits for them, and re-layouts  14.7 us
    dot_general x1, matrix products, dress_left(): jnp.einsum('qin,ia->qan', occ_all, amp_cols, precision=lax.Precision.HIGH...  14.5 us
    all_to_all x3, local copies, waits for them, and re-layouts, shards(): lax.all_to_all(ov_block, 'vec', split_axis=2, concat_axis=0, tiled=True)  7.57 us
    dot_general x2, matrix products, dress_right(): jnp.einsum('qrj,ja->qra', occ_cols, amplitudes, precision=lax.Precision.H...  6.69 us
    add x1, local copies, waits for them, and re-layouts, dress_right(): matrix_rows[:, :, occ_width:] + extra_term  5.96 us
    ppermute x3, waiting for transfers between devices, collected_by_bits(): theirs = lax.ppermute(parts, axis, [(i, i ^ apart) for i in range(peers)])  5.42 us
  transfers between devices with their start and end apart: 5, of which 2 were waited for; matrix products, arithmetic and copies ran while one was open for 23% of the time, Pallas kernels for 0%

profile of v1, /device:TPU:16, one launch (start us, length us, event | category | flops | bytes accessed | tf_op | source)
XLA Modules:
  0.0 141.7 jit_solution(13422900668998691190)
XLA Ops:
  7.2 0.0 all-gather.2.cloned.1.call-start
  7.2 2.3 %copy.10 = f32[11,12,1056]{2,0,1:T(8,128)} copy(f32[11,12,1056]{2,1,0:T(8,128)} %param.3) | data formatting | bytes 1115136 | tf_op args[0]
  9.5 0.0 all-gather.2.cloned.1.call-update
  9.5 0.1 collective-permute-start
  9.6 1.4 %collective-permute-done = f32[1,12,960]{2,1,0:T(8,128)S(1)} collective-permute-done((f32[1,12,960]{2,1,0:T(8,128)}, f32[1,12,960]{2,1,0:T(8,128)S(1)}, u32[]{:S(2)}, u32[]{:S(2)}) %collective-permute-start) | collective-permute-done | bytes 46112 | tf_op jit(solution)/shard_map/ppermute | solution.py:18
  11.0 0.8 pad_maximum_fusion.3
  11.9 1.6 %collective-permute-start.1 = (f32[2,12,960]{2,1,0:T(8,128)S(1)}, f32[2,12,960]{2,1,0:T(8,128)S(1)}, u32[]{:S(2)}, u32[]{:S(2)}) collective-permute-start(f32[2,12,960]{2,1,0:T(8,128)S(1)} %get-tuple-element.4), channel_id=1, source_target_pairs={{0,2},{1,3},{2,0},{3,1},{4,6},{5,7},{6,4},{7,5},{8,10},{9,11},{10,... | collective-permute-start | bytes 276488 | tf_op jit(solution)/shard_map/ppermute | solution.py:18
  13.6 4.0 %collective-permute-done.1 = f32[2,12,960]{2,1,0:T(8,128)S(1)} collective-permute-done((f32[2,12,960]{2,1,0:T(8,128)S(1)}, f32[2,12,960]{2,1,0:T(8,128)S(1)}, u32[]{:S(2)}, u32[]{:S(2)}) %collective-permute-start.1) | collective-permute-done | bytes 92192 | tf_op jit(solution)/shard_map/ppermute | solution.py:18
  17.6 0.2 collective-permute-start.2
  17.8 0.1 fusion.7
  17.9 1.4 multiply_reduce_fusion
  19.3 40.3 %psum.14 = f32[11]{0:T(128)S(1)} all-reduce(f32[11]{0:T(128)S(1)} %multiply_reduce_fusion), channel_id=1, replica_groups=mesh['vec'=4,'orb'=8] {'orb'}, use_global_device_ids=true, to_apply=%region_1.2 | all-reduce | flops 11 | bytes 88 | tf_op jit(solution)/shard_map/psum | solution.py:55
  59.6 0.0 collective-permute-done.2
  59.8 2.0 %fusion.1 = f32[11,12,960]{2,1,0:T(8,128)S(1)} fusion(f32[96,960,1]{1,0,2:T(8,128)S(1)} %reshape.29, f32[11,12,1056]{2,1,0:T(8,128)} %param.3), kind=kOutput, calls=%fused_computation.5 | convolution fusion | flops 146108160 | bytes 1433088 | tf_op jit(solution)/shard_map/qrj,ja->qra/dot_general | solution.py:32
  61.8 6.0 %copy.13 = f32[11,12,960]{1,0,2:T(8,128)} copy(f32[11,12,960]{2,1,0:T(8,128)S(1)} %fusion.1) | data formatting | bytes 1013760 | tf_op jit(solution)/shard_map/add | solution.py:33
  67.7 6.4 %reshape.33 = f32[4,1,31680]{2,1,0:T(1,128)} reshape(f32[960,11,12]{2,1,0:T(8,128)} %bitcast.34) | data formatting | bytes 1013760
  74.1 3.6 %all-to-all-start = ((f32[4,1,31680]{2,1,0:T(1,128)}), f32[4,1,31680]{2,1,0:T(1,128)S(1)}, u32[]{:S(2)}, u32[]{:S(2)}) async-start(f32[4,1,31680]{2,1,0:T(1,128)} %reshape.33), calls=%async_computation | async-start | bytes 1015808 | tf_op jit(solution)/shard_map/all_to_all | solution.py:62
  77.7 0.8 fusion.2
  78.6 18.0 %psum.15 = f32[12,960]{1,0:T(8,128)} all-reduce(f32[12,960]{1,0:T(8,128)S(1)} %bitcast_multiply_fusion), channel_id=1, replica_groups=mesh['vec'=4,'orb'=8] {'vec'}, use_global_device_ids=true, to_apply=%region_2.3 | all-reduce | flops 11520 | bytes 92160 | tf_op jit(solution)/shard_map/psum | solution.py:61
  96.6 0.0 all-to-all-done
  96.6 0.5 broadcast.18
  97.1 2.1 %reduce = f32[4,31680]{1,0:T(4,128)S(1)} reduce(f32[4,1,31680]{2,1,0:T(1,128)S(1)} %all-to-all-done, f32[]{:T(128)} %broadcast.18), dimensions={1}, to_apply=%all_to_all.13.reduce_sub_computation | reduce | bytes 1013764 | tf_op jit(solution)/shard_map/all_to_all | solution.py:62
  99.2 6.0 %reshape.34 = f32[960,11,12]{2,1,0:T(8,128)} reshape(f32[4,31680]{1,0:T(4,128)S(1)} %reduce) | data formatting | bytes 1013760
  105.3 6.2 %copy.14 = f32[11,12,4,240]{3,0,2,1:T(8,128)S(1)} copy(f32[11,12,4,240]{1,0,3,2:T(8,128)} %bitcast.33) | data formatting | bytes 1013760 | tf_op jit(solution)/shard_map/all_to_all | solution.py:62
  111.4 0.9 all_to_all.16
  112.3 0.0 all-gather.2.cloned.1.call-done
  112.3 14.5 %bitcast_subtract_fusion = f32[11,120,1056]{1,2,0:T(8,128)S(1)} fusion(f32[11,120,1056]{1,2,0:T(8,128)} %param.4, f32[11,96,1056]{2,0,1:T(8,128)} %all-gather.2.cloned.1.call-done, f32[96,960]{1,0:T(8,128)S(1)} %reshape_reshape.3, s32[]{:T(128)S(6)} %select_n.41), kind=kOutput, calls=%fused_computation.1 | convolution fusion | flops 1607189760 | bytes 15661060 | tf_op jit(solution)/shard_map/qin,ia->qan/dot_general | solution.py:37
  126.9 4.7 %slice_add_fusion = f32[11,120,960]{1,2,0:T(8,128)S(1)} fusion(f32[11,120,1056]{1,2,0:T(8,128)S(1)} %bitcast_subtract_fusion, f32[96,960,1]{1,0,2:T(8,128)S(1)} %reshape.29), kind=kOutput, calls=%fused_computation.2 | convolution fusion | flops 1461081600 | bytes 11013120 | tf_op jit(solution)/shard_map/qrj,ja->qra/dot_general | solution.py:32
  131.7 3.2 %pad_maximum_fusion = f32[11,120,1056]{1,2,0:T(8,128)} fusion(f32[11,120,960]{1,2,0:T(8,128)S(1)} %slice_add_fusion, f32[11,120,96]{1,2,0:T(8,128)S(1)} %slice.16), kind=kLoop, calls=%fused_computation | loop fusion | flops 1393920 | bytes 11151360 | tf_op jit(solution)/shard_map/concatenate | solution.py:33
  (10 shorter events, 0.3 us)
Async XLA Ops:
  7.2 105.2 %all-gather.2.cloned.1.call-start = ((), (), s32[]{:S(2)}) async-start(), calls=%async_computation.1 | async-start | bytes 7962624 | tf_op jit(solution)/shard_map/all_gather | solution.py:46
  9.5 1.5 %collective-permute-start = (f32[1,12,960]{2,1,0:T(8,128)}, f32[1,12,960]{2,1,0:T(8,128)S(1)}, u32[]{:S(2)}, u32[]{:S(2)}) collective-permute-start(f32[1,12,960]{2,1,0:T(8,128)} %bitcast.40), channel_id=1, source_target_pairs={{0,1},{1,0},{2,3},{3,2},{4,5},{5,4},{6,7},{7,6},{8,9},{9,8},{10,11... | collective-permute-start | bytes 138248 | tf_op jit(solution)/shard_map/ppermute | solution.py:18
  11.9 5.6 %collective-permute-start.1 = (f32[2,12,960]{2,1,0:T(8,128)S(1)}, f32[2,12,960]{2,1,0:T(8,128)S(1)}, u32[]{:S(2)}, u32[]{:S(2)}) collective-permute-start(f32[2,12,960]{2,1,0:T(8,128)S(1)} %get-tuple-element.4), channel_id=1, source_target_pairs={{0,2},{1,3},{2,0},{3,1},{4,6},{5,7},{6,4},{7,5},{8,10},{9,11},{10,... | collective-permute-start | bytes 276488 | tf_op jit(solution)/shard_map/ppermute | solution.py:18
  17.6 42.0 %collective-permute-start.2 = (f32[4,12,960]{2,1,0:T(8,128)S(1)}, f32[4,12,960]{2,1,0:T(8,128)S(1)}, u32[]{:S(2)}, u32[]{:S(2)}) collective-permute-start(f32[4,12,960]{2,1,0:T(8,128)S(1)} %bitcast.36), channel_id=1, source_target_pairs={{0,4},{1,5},{2,6},{3,7},{4,0},{5,1},{6,2},{7,3},{8,12},{9,13},{10,... | collective-permute-start | bytes 552968 | tf_op jit(solution)/shard_map/ppermute | solution.py:18
  74.1 22.4 %all-to-all-start = ((f32[4,1,31680]{2,1,0:T(1,128)}), f32[4,1,31680]{2,1,0:T(1,128)S(1)}, u32[]{:S(2)}, u32[]{:S(2)}) async-start(f32[4,1,31680]{2,1,0:T(1,128)} %reshape.33), calls=%async_computation | async-start | bytes 1015808 | tf_op jit(solution)/shard_map/all_to_all | solution.py:62
Sparse Core Ops, SparseCore 0:
  10.2 76.0 all-gather.1
